TPU v7x, 256 devices: a whole 4x4x8 slice. The times are simulated.
256 devices in a mesh: tile: 64 (over z, x, core), rot: 4 (over y).
Axes of the slice: x: 4, y: 4, z: 8, core: 2. Of those that a mesh axis runs over, the one named last changes fastest.
Arguments:
- tomogram: bfloat16 [2048, 5120], P('tile'), may hold values from -12 to 12
- templates: bfloat16 [16, 110592], P('rot', 'tile'), may hold values from -6 to 6
- valid: int32 [2048, 80], P('tile'), may hold values from 0 to 1, as said below
- quats: float32 [4, 4096], replicated, may hold values from -1 to 1, as said below
- rot_index: int32 [16], P('rot'), may hold values from 0 to 4095
Outputs:
- best: float32 [2048, 5120], P('tile', 'rot')
- evidence: float32 [2048, 5120], P('tile', 'rot')
- moments: float32 [4, 2048, 5120], P(None, 'tile', 'rot')
Inputs may be any that keep to these rules, and one draw needn't show every extreme that they name: `valid`: 1 marks a column (x, y) of voxels inside the lamella. `quats`: each column is a unit quaternion with a non-negative first component.
All inputs are finite; a program needn't handle non-finite values.
Results may differ from a plain program's by a relative error of at most 0.0003.
Values may be sent and summed in bfloat16 or wider, within the bound.
A program may use at most 128 MiB of HBM per device.

v0:
```python
import math
import jax
import jax.numpy as jnp
from jax import lax
from jax.sharding import PartitionSpec as P

TEMPL = 48
HALF = 24
EPSILON = 1e-06
TWO_PI = 2.0 * math.pi


def padded(block, sides, width):
    for axis, dim in sides:
        count = lax.axis_size(axis)
        forward = [(i, i + 1) for i in range(count - 1)]
        backward = [(target, source) for source, target in forward]
        low = lax.ppermute(
            lax.slice_in_dim(block, block.shape[dim] - width, None, axis=dim), axis, forward
        )
        high = lax.ppermute(lax.slice_in_dim(block, 0, width, axis=dim), axis, backward)
        block = jnp.concatenate([low, block, high], axis=dim)
    return block


def twiddle(count_in, shift_in, count_out, shift_out, length, direction, factor):
    row_idx = (jnp.arange(count_in, dtype=jnp.int32) + shift_in)[:, None]
    col_idx = (jnp.arange(count_out, dtype=jnp.int32) + shift_out)[None, :]
    phase_idx = jnp.remainder(row_idx * col_idx, length).astype(jnp.float32)
    angles = phase_idx * jnp.float32(direction * TWO_PI / length)
    real_part = jnp.cos(angles) * factor
    imag_part = jnp.sin(angles) * factor
    upper_half = jnp.stack([real_part, imag_part], axis=1)
    lower_half = jnp.stack([-imag_part, real_part], axis=1)
    return jnp.stack([upper_half, lower_half], axis=0)


def product(formula, left_arr, right_arr):
    return jnp.einsum(
        formula,
        left_arr,
        right_arr,
        precision=lax.Precision.HIGH,
        preferred_element_type=jnp.float32,
    )


def forward(volume, shift, direction, lengths):
    size_x, size_y, size_z = volume.shape
    table_z = twiddle(size_z, shift, lengths[2], 0, lengths[2], direction, 1.0)[0]
    spectrum = product("xyz,zdk->dxyk", volume, table_z)
    spectrum = product(
        "cxyz,cydk->dxkz",
        spectrum,
        twiddle(size_y, shift, lengths[1], 0, lengths[1], direction, 1.0),
    )
    return product(
        "cxyz,cxdk->dkyz",
        spectrum,
        twiddle(size_x, shift, lengths[0], 0, lengths[0], direction, 1.0),
    )


def inverse(spectrum, out_x, out_y, out_z, lengths):
    spectrum = product(
        "cxyz,cxdk->dkyz",
        spectrum,
        twiddle(lengths[0], 0, out_x, HALF, lengths[0], 1, 1.0 / lengths[0]),
    )
    spectrum = product(
        "cxyz,cydk->dxkz",
        spectrum,
        twiddle(lengths[1], 0, out_y, 0, lengths[1], 1, 1.0 / lengths[1]),
    )
    real_table = twiddle(lengths[2], 0, out_z, 0, lengths[2], 1, 1.0 / lengths[2])[:, :, 0]
    return product("cxyz,czk->xyk", spectrum, real_table)


def multiply(first_arr, other_arr):
    return jnp.stack(
        [
            first_arr[0] * other_arr[0] - first_arr[1] * other_arr[1],
            first_arr[0] * other_arr[1] + first_arr[1] * other_arr[0],
        ]
    )


def local(tomogram, templates, valid, quats, rot_index):
    x_cells, voxels = tomogram.shape
    y_cells = valid.shape[1]
    z_cells = voxels // y_cells
    lengths = (x_cells + TEMPL, y_cells + HALF, z_cells + HALF)
    widened = padded(tomogram, (("tile", 0),), HALF)
    slab_spectrum = forward(
        widened.astype(jnp.float32).reshape(x_cells + TEMPL, y_cells, z_cells), 0, -1, lengths
    )
    gathered_bank = lax.all_gather(templates, "tile", axis=1, tiled=True).astype(jnp.float32)
    centred = gathered_bank - jnp.mean(gathered_bank, axis=1, keepdims=True)
    tmpl_spread = jnp.sqrt(jnp.mean(centred * centred, axis=1, keepdims=True) + EPSILON)
    unit_bank = centred / (tmpl_spread * jnp.float32(TEMPL) ** 1.5)

    def correlate(unit_tmpl):
        tmpl_spectrum = forward(unit_tmpl.reshape(TEMPL, TEMPL, TEMPL), -HALF, 1, lengths)
        return inverse(multiply(slab_spectrum, tmpl_spectrum), x_cells, y_cells, z_cells, lengths)

    correlation = lax.map(correlate, unit_bank).reshape(unit_bank.shape[0], x_cells, voxels)
    inside = jnp.repeat(valid.astype(jnp.float32), z_cells, axis=1)
    columns = jnp.sum(valid.astype(jnp.float32))
    masked = correlation * inside[None]
    first_sum, all_columns = lax.psum((jnp.sum(masked, axis=(1, 2)), columns), "tile")
    voxel_count = all_columns * z_cells
    average = first_sum / voxel_count
    deviation = correlation - average[:, None, None]
    square_sum = lax.psum(jnp.sum(inside[None] * deviation * deviation, axis=(1, 2)), "tile")
    spread = jnp.sqrt(square_sum / voxel_count + EPSILON)
    scores = (correlation - average[:, None, None]) / spread[:, None, None]
    one_hot = (rot_index[:, None] == jnp.arange(quats.shape[1], dtype=jnp.int32)[None, :]).astype(
        jnp.float32
    )
    orient = product("rq,kq->rk", one_hot, quats)
    highest = jnp.max(scores, axis=0)
    weight = jnp.exp(scores - highest[None])
    exp_total = jnp.sum(weight, axis=0)
    moment = product("rxv,rk->kxv", weight, orient)
    groups = lax.axis_size("rot")
    share_len = voxels // groups
    offset = lax.axis_index("rot") * share_len
    high_full = lax.pmax(highest, "rot")
    rescale = jnp.exp(highest - high_full)
    total_full, moment_full = lax.psum((exp_total * rescale, moment * rescale[None]), "rot")
    high_all = lax.dynamic_slice_in_dim(high_full, offset, share_len, 1)
    total_all = lax.dynamic_slice_in_dim(total_full, offset, share_len, 1)
    moment_all = lax.dynamic_slice_in_dim(moment_full, offset, share_len, 2)
    inside_part = lax.dynamic_slice_in_dim(inside, offset, share_len, 1)
    best = inside_part * high_all
    evidence = inside_part * (high_all + jnp.log(total_all))
    moments = inside_part[None] * moment_all / total_all[None]
    return (best, evidence, moments)


def solution(mesh):
    placed = (P("tile", None), P("rot", "tile"), P("tile", None), P(), P("rot"))
    return jax.shard_map(
        local,
        mesh=mesh,
        in_specs=placed,
        out_specs=(P("tile", "rot"), P("tile", "rot"), P(None, "tile", "rot")),
        check_vma=False,
    )
```

profile of v0, /device:TPU:1, one launch (start us, length us, event | category | flops | bytes accessed | tf_op | source)
XLA Modules:
  0.0 683.0 jit_solution(3317119279552520776)
XLA Ops:
  7.2 1.8 fusion.124
  9.0 4.5 collective-permute-start
  13.5 1.9 collective-permute-start.1
  16.4 55.7 %all-gather = bf16[64,1728,4]{1,2,0:T(4,128)(2,1)S(1)} all-gather(bf16[1,1728,4]{1,2,0:T(4,128)(2,1)} %bitcast.196), channel_id=1, replica_groups=mesh['tile'=64,'rot'=4] {'tile'}, dimensions={0}, use_global_device_ids=true | all-gather | bytes 898560 | tf_op jit(solution)/shard_map/all_gather | solution.py:97
  74.6 2.8 reshape.771
  78.5 1.6 divide_bitcast_fusion
  82.6 1.5 reshape.767
  84.1 4.6 convolution_bitcast_fusion.1
  88.8 9.4 %copy.71 = f32[2,80,80,88,1]{2,1,0,4,3:T(8,128)} copy(f32[2,80,80,88,1]{3,2,1,0,4:T(8,128)} %convolution_bitcast_fusion.1) | data formatting | bytes 9011200 | tf_op jit(solution)/shard_map/xyz,zdk->dxyk/transpose | solution.py:39
  98.2 5.5 fusion.90
  103.7 5.6 fusion.83
  109.3 145.3 %while.13 = (s32[]{:T(128)}, f32[4,32,80,64]{2,3,1,0:T(8,128)}, f32[2,80,104,88]{2,1,3,0:T(8,128)}, f32[4,110592]{1,0:T(4,128)}, s32[]{:T(128)}) while((s32[]{:T(128)}, f32[4,32,80,64]{2,3,1,0:T(8,128)}, f32[2,80,104,88]{2,1,3,0:T(8,128)}, f32[4,110592]{1,0:T(4,128)}, s32[]{:T(128)}) %tuple.86), condition=%wide.region_3.4_spmd, body=%wide.region_2.3_spmd.sunk | while | flops 2770436608 | bytes 55842368 | solution.py:106
  109.6 2.8 dynamic-slice_reduce_fusion.2
  112.4 1.5 reshape.806
  114.1 2.3 convolution_bitcast_fusion.4
  116.4 4.6 copy.104
  121.0 3.8 fusion.158
  125.1 3.1 fusion.160
  128.1 5.9 multiply_subtract_fusion.2
  134.2 4.5 fusion.161
  139.1 3.5 fusion.163
  143.0 2.7 fusion.165
  145.9 2.8 dynamic-slice_reduce_fusion.2
  148.6 1.5 reshape.806
  150.3 2.3 convolution_bitcast_fusion.4
  152.7 4.6 copy.104
  157.2 3.8 fusion.158
  161.3 3.1 fusion.160
  164.4 5.9 multiply_subtract_fusion.2
  170.5 4.5 fusion.161
  175.4 3.5 fusion.163
  179.2 2.7 fusion.165
  182.1 2.8 dynamic-slice_reduce_fusion.2
  186.6 2.3 convolution_bitcast_fusion.4
  188.9 4.6 copy.104
  193.5 3.8 fusion.158
  197.5 3.1 fusion.160
  200.6 5.9 multiply_subtract_fusion.2
  206.7 4.5 fusion.161
  211.6 3.5 fusion.163
  215.4 2.7 fusion.165
  218.4 2.8 dynamic-slice_reduce_fusion.2
  222.8 2.3 convolution_bitcast_fusion.4
  225.1 4.6 copy.104
  229.7 3.8 fusion.158
  233.8 3.1 fusion.160
  236.8 5.9 multiply_subtract_fusion.2
  242.9 4.5 fusion.161
  247.8 3.5 fusion.163
  251.7 2.7 fusion.165
  254.6 2.8 multiply_reduce_fusion
  257.7 124.2 %all-reduce = (f32[4]{0:T(128)S(1)}, f32[]{:T(128)}) all-reduce(f32[4]{0:T(128)S(1)} %multiply_reduce_fusion, f32[]{:T(128)} %convert_reduce_fusion.1), channel_id=1, replica_groups=mesh['tile'=64,'rot'=4] {'tile'}, use_global_device_ids=true, to_apply=%region_5.6 | all-reduce | flops 5 | bytes 40 | tf_op jit(solution)/shard_map/psum | solution.py:110
  382.6 3.1 fusion.82
  385.7 5.7 copy.55
  391.4 126.6 %psum.37 = f32[4]{0:T(128)S(1)} all-reduce(f32[4]{0:T(128)S(1)} %fusion.82), channel_id=1, replica_groups=mesh['tile'=64,'rot'=4] {'tile'}, use_global_device_ids=true, to_apply=%region_9.10 | all-reduce | flops 4 | bytes 32 | tf_op jit(solution)/shard_map/psum | solution.py:114
  518.1 3.0 fusion.122
  521.5 4.4 exponential_reduce_fusion
  527.1 5.4 reshape.768
  534.2 2.2 subtract_exponential_fusion
  536.5 41.4 %all-reduce.5.cloned.1.call-done = f32[32,5120]{1,0:T(8,128)} async-done(((f32[32,5120]{1,0:T(8,128)}), f32[32,5120]{1,0:T(8,128)}) %all-reduce.5.cloned.1.call-update) | async-done | bytes 655376 | tf_op jit(solution)/shard_map/pmax | solution.py:128
  577.9 2.2 fusion.123
  580.1 5.6 convolution_multiply_fusion
  586.6 85.2 %all-reduce.7.cloned.1.call-done = (f32[32,5120]{1,0:T(8,128)}, f32[4,32,5120]{2,0,1:T(4,128)}) async-done(((f32[32,5120]{1,0:T(8,128)}, f32[4,32,5120]{2,0,1:T(4,128)}), (f32[32,5120]{1,0:T(8,128)}, f32[4,32,5120]{2,0,1:T(4,128)})) %all-reduce.7.cloned.1.call-update) | async-done | bytes 3276816 | tf_op jit(solution)/shard_map/psum | solution.py:130
  671.7 1.8 add_multiply_fusion
  (109 shorter events, 22.4 us)
Async XLA Ops:
  7.2 250.3 %copy-start = (f32[4,4096]{1,0:T(4,128)S(1)}, f32[4,4096]{1,0:T(4,128)}, u32[]{:S(2)}) copy-start(f32[4,4096]{1,0:T(4,128)} %param.10) | copy-start | bytes 196612
  7.2 570.7 %all-reduce.5.cloned.1.call-start = ((), (), s32[]{:S(2)}) async-start(), calls=%async_computation | async-start | bytes 1310720 | tf_op jit(solution)/shard_map/pmax | solution.py:128
  9.0 71.8 %collective-permute-start = (bf16[24,5120]{1,0:T(8,128)(2,1)}, bf16[24,5120]{1,0:T(8,128)(2,1)S(1)}, u32[]{:S(2)}, u32[]{:S(2)}) collective-permute-start(bf16[24,5120]{1,0:T(8,128)(2,1)} %get-tuple-element.138), channel_id=1, source_target_pairs={{0,4},{4,8},{8,12},{12,16},{16,20},{20,24},{24,28},{28,32},{32,36}... | collective-permute-start | bytes 737288 | tf_op jit(solution)/shard_map/ppermute | solution.py:18
  13.5 68.0 %collective-permute-start.1 = (bf16[24,5120]{1,0:T(8,128)(2,1)S(1)}, bf16[24,5120]{1,0:T(8,128)(2,1)}, u32[]{:S(2)}, u32[]{:S(2)}) collective-permute-start(bf16[24,5120]{1,0:T(8,128)(2,1)S(1)} %get-tuple-element.139), channel_id=1, source_target_pairs={{4,0},{8,4},{12,8},{16,12},{20,16},{24,20},{28,24},{32,28},{36,32}... | collective-permute-start | bytes 737288 | tf_op jit(solution)/shard_map/ppermute | solution.py:21
  74.6 5.6 copy-start.5
  77.4 4.1 copy-start.3
  80.8 0.7 copy-start.4
  254.6 2.9 copy-start.6
  527.1 5.4 copy-start.2
  532.5 1.7 copy-start.1
  534.2 137.5 %all-reduce.7.cloned.1.call-start = ((), (), s32[]{:S(2)}) async-start(), calls=%async_computation.1 | async-start | bytes 6553600 | tf_op jit(solution)/shard_map/psum | solution.py:130
Sparse Core Ops, SparseCore 0:
  534.3 43.5 all-reduce.4
  585.9 85.7 all-reduce.6
where the time goes:
time: 690 us; the launch traced here: 683 us
  blocking collectives  307 us (44%)
  waiting for transfers between devices  127 us (18%)
  matrix products  101 us (15%)
  local copies, waits for them, and re-layouts  69.1 us (10%)
  other arithmetic  56.8 us (8%)
  between operations  15.3 us (2%)
    psum x1, blocking collectives, local(): lax.psum(jnp.sum(inside[None] * deviation * deviation, axis=(1, 2)), 'tile')  127 us
    psum x1, blocking collectives, local(): lax.psum((jnp.sum(masked, axis=(1, 2)), columns), 'tile')  124 us
    dot_general x29, matrix products, product(): jnp.einsum(formula, left_arr, right_arr, precision=lax.Precision.HIGH, pr...  101 us
    psum x1, waiting for transfers between devices, local(): lax.psum((exp_total * rescale, moment * rescale[None]), 'rot')  85.2 us
    all_gather x1, blocking collectives, local(): lax.all_gather(templates, 'tile', axis=1, tiled=True).astype(jnp.float32)  55.7 us
    pmax x1, waiting for transfers between devices, local(): high_full = lax.pmax(highest, 'rot')  41.4 us
    transpose x5, local copies, waits for them, and re-layouts, product(): jnp.einsum(formula, left_arr, right_arr, precision=lax.Precision.HIGH, pr...  27.7 us
    sub x4, other arithmetic, multiply(): first_arr[0] * other_arr[0] - first_arr[1] * other_arr[1]  23.7 us
  transfers between devices with their start and end apart: 4, of which 2 were waited for; matrix products, arithmetic and copies ran while one was open for 2% of the time, Pallas kernels for 0%

commit v1 on v0

--- a/solution.py
+++ b/solution.py
@@ -86,6 +86,15 @@
 
 
 def local(tomogram, templates, valid, quats, rot_index):
+
+    def unite_column(inputs, axis_id):
+        n_peers_all = lax.axis_size(axis_id)
+        next_value = jnp.tile(inputs, [n_peers_all if k0 == 1 else 1 for k0 in range(inputs.ndim)])
+        plain = lax.all_to_all(
+            next_value, axis_name=axis_id, split_axis=1, concat_axis=1, tiled=True
+        )
+        return plain
+
     x_cells, voxels = tomogram.shape
     y_cells = valid.shape[1]
     z_cells = voxels // y_cells
@@ -94,7 +103,7 @@
     slab_spectrum = forward(
         widened.astype(jnp.float32).reshape(x_cells + TEMPL, y_cells, z_cells), 0, -1, lengths
     )
-    gathered_bank = lax.all_gather(templates, "tile", axis=1, tiled=True).astype(jnp.float32)
+    gathered_bank = unite_column(templates, axis_id="tile").astype(jnp.float32)
     centred = gathered_bank - jnp.mean(gathered_bank, axis=1, keepdims=True)
     tmpl_spread = jnp.sqrt(jnp.mean(centred * centred, axis=1, keepdims=True) + EPSILON)
     unit_bank = centred / (tmpl_spread * jnp.float32(TEMPL) ** 1.5)

time: 690 us -> 659 us (0.955)
  blocking collectives: 307 us -> 253 us
  starting transfers between devices: 6.52 us -> 19.5 us
  loops' own time: 0.79 us -> 12.2 us
  local copies, waits for them, and re-layouts: 69.1 us -> 61.9 us
    all_gather x1 -> x0, blocking collectives: 55.7 us -> none  [local(): lax.all_gather(templates, 'tile', axis=1, tiled=True).astype(jnp.float32)]
    all_to_all x0 -> x1, starting transfers between devices: none -> 13 us  [unite_column(): lax.all_to_all(next_value, axis_name=axis_id, split_axis=1, concat_axis=1...]
    another operation x1, loops' own time: 0.79 us -> 12.2 us  [local(): lax.map(correlate, unit_bank).reshape(unit_bank.shape[0], x_cells, voxels)]
  transfers between devices with their start and end apart: 4 -> 5, of which waited for: 2 -> 2; matrix products, arithmetic and copies ran while one was open for 2% -> 5% of each run, Pallas kernels for 0% -> 0%
where the time goes in v1:
time: 659 us; the launch traced here: 649 us
  blocking collectives  253 us (38%)
  waiting for transfers between devices  126 us (19%)
  matrix products  102 us (15%)
  local copies, waits for them, and re-layouts  61.9 us (9%)
  other arithmetic  58 us (9%)
  starting transfers between devices  19.5 us (3%)
  between operations  15.3 us (2%)
  loops' own time  12.2 us (2%)
    psum x1, blocking collectives, local(): lax.psum(jnp.sum(inside[None] * deviation * deviation, axis=(1, 2)), 'tile')  129 us
    psum x1, blocking collectives, local(): lax.psum((jnp.sum(masked, axis=(1, 2)), columns), 'tile')  125 us
    dot_general x29, matrix products, product(): jnp.einsum(formula, left_arr, right_arr, precision=lax.Precision.HIGH, pr...  102 us
    psum x1, waiting for transfers between devices, local(): lax.psum((exp_total * rescale, moment * rescale[None]), 'rot')  85.2 us
    pmax x1, waiting for transfers between devices, local(): high_full = lax.pmax(highest, 'rot')  41.1 us
    transpose x5, local copies, waits for them, and re-layouts, product(): jnp.einsum(formula, left_arr, right_arr, precision=lax.Precision.HIGH, pr...  27.7 us
    sub x4, other arithmetic, multiply(): first_arr[0] * other_arr[0] - first_arr[1] * other_arr[1]  23.6 us
  transfers between devices with their start and end apart: 5, of which 2 were waited for; matrix products, arithmetic and copies ran while one was open for 5% of the time, Pallas kernels for 0%

profile of v1, /device:TPU:1, one launch (start us, length us, event | category | flops | bytes accessed | tf_op | source)
XLA Modules:
  0.0 648.7 jit_solution(13567034579072992435)
XLA Ops:
  8.4 4.5 collective-permute-start
  12.9 1.9 collective-permute-start.1
  14.8 1.9 tile.2
  16.7 13.0 %all-to-all-start = ((bf16[4,64,1728]{2,0,1:T(4,128)(2,1)}), bf16[4,64,1728]{2,0,1:T(4,128)(2,1)S(1)}, u32[]{:S(2)}, u32[]{:S(2)}) async-start(bf16[4,64,1728]{2,0,1:T(4,128)(2,1)} %tile.2), calls=%async_computation | async-start | bytes 1835008 | tf_op jit(solution)/shard_map/all_to_all | solution.py:93
  34.4 5.4 convolution_bitcast_fusion.1
  39.8 9.4 %copy.69 = f32[2,80,80,88,1]{2,1,0,4,3:T(8,128)} copy(f32[2,80,80,88,1]{3,2,1,0,4:T(8,128)} %convolution_bitcast_fusion.1) | data formatting | bytes 9011200 | tf_op jit(solution)/shard_map/xyz,zdk->dxyk/transpose | solution.py:39
  49.2 5.5 fusion.90
  54.8 5.6 fusion.83
  62.8 2.6 reshape.783
  65.4 1.8 subtract_divide_fusion.1
  67.3 150.8 %while.13 = (s32[]{:T(128)}, f32[4,32,80,64]{2,3,1,0:T(8,128)}, f32[2,80,104,88]{2,1,3,0:T(8,128)}, f32[4,110592]{1,0:T(4,128)S(1)}, s32[]{:T(128)}) while((s32[]{:T(128)}, f32[4,32,80,64]{2,3,1,0:T(8,128)}, f32[2,80,104,88]{2,1,3,0:T(8,128)}, f32[4,110592]{1,0:T(4,128)S(1)}, s32[]{:T(128)}) %tuple.86), condition=%wide.region_3.4_spmd, body=%wide.region_2.3_spmd.sunk | while | flops 2770436608 | bytes 69998200 | solution.py:115
  79.1 1.3 dynamic-slice_reduce_fusion.2
  80.4 1.5 reshape.818
  82.1 2.3 convolution_bitcast_fusion.4
  84.4 4.6 copy.102
  89.0 3.8 fusion.158
  93.1 3.1 fusion.160
  96.1 5.9 multiply_subtract_fusion.2
  102.2 4.5 fusion.161
  107.1 3.5 fusion.163
  111.0 2.7 fusion.165
  115.1 1.5 reshape.818
  116.9 2.3 convolution_bitcast_fusion.4
  119.2 4.6 copy.102
  123.8 3.8 fusion.158
  127.8 3.1 fusion.160
  130.9 5.9 multiply_subtract_fusion.2
  137.0 4.5 fusion.161
  141.9 3.5 fusion.163
  145.7 2.7 fusion.165
  149.9 1.5 reshape.818
  151.7 2.3 convolution_bitcast_fusion.4
  154.0 4.6 copy.102
  158.6 3.8 fusion.158
  162.6 3.1 fusion.160
  165.7 5.9 multiply_subtract_fusion.2
  171.8 4.5 fusion.161
  176.7 3.5 fusion.163
  180.5 2.7 fusion.165
  183.5 1.3 dynamic-slice_reduce_fusion.2
  184.7 1.5 reshape.818
  186.4 2.3 convolution_bitcast_fusion.4
  188.8 4.6 copy.102
  193.4 3.8 fusion.158
  197.4 3.1 fusion.160
  200.5 5.9 multiply_subtract_fusion.2
  206.6 4.5 fusion.161
  211.5 3.5 fusion.163
  215.3 2.7 fusion.165
  218.1 2.8 multiply_reduce_fusion
  221.2 124.6 %all-reduce = (f32[4]{0:T(128)S(1)}, f32[]{:T(128)}) all-reduce(f32[4]{0:T(128)S(1)} %multiply_reduce_fusion, f32[]{:T(128)} %convert_reduce_fusion.1), channel_id=1, replica_groups=mesh['tile'=64,'rot'=4] {'tile'}, use_global_device_ids=true, to_apply=%region_5.6 | all-reduce | flops 5 | bytes 40 | tf_op jit(solution)/shard_map/psum | solution.py:119
  346.4 3.1 fusion.82
  349.6 5.7 copy.53
  355.2 128.7 %psum.37 = f32[4]{0:T(128)S(1)} all-reduce(f32[4]{0:T(128)S(1)} %fusion.82), channel_id=1, replica_groups=mesh['tile'=64,'rot'=4] {'tile'}, use_global_device_ids=true, to_apply=%region_9.10 | all-reduce | flops 4 | bytes 32 | tf_op jit(solution)/shard_map/psum | solution.py:123
  484.0 3.0 fusion.122
  487.4 4.4 exponential_reduce_fusion
  493.0 5.4 reshape.782
  500.2 2.2 subtract_exponential_fusion
  502.4 41.1 %all-reduce.5.cloned.1.call-done = f32[32,5120]{1,0:T(8,128)} async-done(((f32[32,5120]{1,0:T(8,128)}), f32[32,5120]{1,0:T(8,128)}) %all-reduce.5.cloned.1.call-update) | async-done | bytes 655376 | tf_op jit(solution)/shard_map/pmax | solution.py:137
  543.6 2.2 fusion.123
  545.8 5.6 convolution_multiply_fusion
  552.2 85.2 %all-reduce.7.cloned.1.call-done = (f32[32,5120]{1,0:T(8,128)}, f32[4,32,5120]{2,0,1:T(4,128)}) async-done(((f32[32,5120]{1,0:T(8,128)}, f32[4,32,5120]{2,0,1:T(4,128)}), (f32[32,5120]{1,0:T(8,128)}, f32[4,32,5120]{2,0,1:T(4,128)})) %all-reduce.7.cloned.1.call-update) | async-done | bytes 3276816 | tf_op jit(solution)/shard_map/psum | solution.py:139
  637.4 1.8 add_multiply_fusion
  639.2 1.3 multiply_divide_fusion
  (131 shorter events, 21.9 us)
Async XLA Ops:
  7.2 213.7 %copy-start = (f32[4,4096]{1,0:T(4,128)S(1)}, f32[4,4096]{1,0:T(4,128)}, u32[]{:S(2)}) copy-start(f32[4,4096]{1,0:T(4,128)} %param.10) | copy-start | bytes 196612
  7.2 26.1 %copy-start.5 = (bf16[32,5120]{1,0:T(8,128)(2,1)S(1)}, bf16[32,5120]{1,0:T(8,128)(2,1)}, u32[]{:S(2)}) copy-start(bf16[32,5120]{1,0:T(8,128)(2,1)} %param.7) | copy-start | bytes 983044
  7.2 24.1 %copy-start.9 = (s32[32,80]{1,0:T(8,128)S(1)}, s32[32,80]{1,0:T(8,128)}, u32[]{:S(2)}) copy-start(s32[32,80]{1,0:T(8,128)} %param.9) | copy-start | bytes 30724
  8.4 24.9 %collective-permute-start = (bf16[24,5120]{1,0:T(8,128)(2,1)S(1)}, bf16[24,5120]{1,0:T(8,128)(2,1)S(1)}, u32[]{:S(2)}, u32[]{:S(2)}) collective-permute-start(bf16[24,5120]{1,0:T(8,128)(2,1)S(1)} %get-tuple-element.138), channel_id=1, source_target_pairs={{0,4},{4,8},{8,12},{12,16},{16,20},{20,24},{24,28},{28,32},{32,36}... | collective-permute-start | bytes 737288 | tf_op jit(solution)/shard_map/ppermute | solution.py:18
  12.9 20.4 %collective-permute-start.1 = (bf16[24,5120]{1,0:T(8,128)(2,1)S(1)}, bf16[24,5120]{1,0:T(8,128)(2,1)S(1)}, u32[]{:S(2)}, u32[]{:S(2)}) collective-permute-start(bf16[24,5120]{1,0:T(8,128)(2,1)S(1)} %get-tuple-element.139), channel_id=1, source_target_pairs={{4,0},{8,4},{12,8},{16,12},{20,16},{24,20},{28,24},{32,28},{36,32}... | collective-permute-start | bytes 737288 | tf_op jit(solution)/shard_map/ppermute | solution.py:21
  16.7 43.7 %all-to-all-start = ((bf16[4,64,1728]{2,0,1:T(4,128)(2,1)}), bf16[4,64,1728]{2,0,1:T(4,128)(2,1)S(1)}, u32[]{:S(2)}, u32[]{:S(2)}) async-start(bf16[4,64,1728]{2,0,1:T(4,128)(2,1)} %tile.2), calls=%async_computation | async-start | bytes 1835008 | tf_op jit(solution)/shard_map/all_to_all | solution.py:93
  29.7 513.8 %all-reduce.5.cloned.1.call-start = ((), (), s32[]{:S(2)}) async-start(), calls=%async_computation.1 | async-start | bytes 1310720 | tf_op jit(solution)/shard_map/pmax | solution.py:137
  39.8 9.4 %copy-start.6 = (f32[1,80,2,104]{3,1,0,2:T(8,128)S(1)}, f32[1,80,2,104]{3,1,0,2:T(8,128)}, u32[]{:S(2)}) copy-start(f32[1,80,2,104]{3,1,0,2:T(8,128)} %get-tuple-element.143) | copy-start | bytes 199684
  49.2 5.6 copy-start.7
  49.2 5.6 copy-start.8
  78.9 3.2 copy-start.2
  107.1 6.5 %copy-start.3 = (f32[4,110592]{1,0:T(4,128)S(1)}, f32[4,110592]{1,0:T(4,128)}, u32[]{:S(2)}) copy-start(f32[4,110592]{1,0:T(4,128)} %copy-done.2) | copy-start | bytes 5308420 | tf_op jit(solution)/shard_map/while
  113.7 3.2 copy-start.2
  141.9 6.6 %copy-start.3 = (f32[4,110592]{1,0:T(4,128)S(1)}, f32[4,110592]{1,0:T(4,128)}, u32[]{:S(2)}) copy-start(f32[4,110592]{1,0:T(4,128)} %copy-done.2) | copy-start | bytes 5308420 | tf_op jit(solution)/shard_map/while
  148.5 3.2 copy-start.2
  176.7 6.6 %copy-start.3 = (f32[4,110592]{1,0:T(4,128)S(1)}, f32[4,110592]{1,0:T(4,128)}, u32[]{:S(2)}) copy-start(f32[4,110592]{1,0:T(4,128)} %copy-done.2) | copy-start | bytes 5308420 | tf_op jit(solution)/shard_map/while
  183.3 3.2 copy-start.2
  211.5 6.6 %copy-start.3 = (f32[4,110592]{1,0:T(4,128)S(1)}, f32[4,110592]{1,0:T(4,128)}, u32[]{:S(2)}) copy-start(f32[4,110592]{1,0:T(4,128)} %copy-done.2) | copy-start | bytes 5308420 | tf_op jit(solution)/shard_map/while
  218.1 2.9 copy-start.10
  493.0 5.4 copy-start.4
  498.4 1.7 copy-start.1
  500.1 137.3 %all-reduce.7.cloned.1.call-start = ((), (), s32[]{:S(2)}) async-start(), calls=%async_computation.2 | async-start | bytes 6553600 | tf_op jit(solution)/shard_map/psum | solution.py:139
Sparse Core Ops, SparseCore 0:
  500.2 43.2 all-reduce.4
  551.6 85.7 all-reduce.6
